TPU v7x, 256 devices: a whole 4x4x8 slice. The times are simulated.
256 devices in a mesh: pole: 4 (over y), row: 8 (over z_lo, x), col: 8 (over z_hi, core).
Axes of the slice: x: 4, y: 4, z: 8 (z_hi: 4, z_lo: 2; z = z_hi * 2 + z_lo), core: 2. Of those that a mesh axis runs over, the one named last changes fastest.
Arguments:
- found_inverse: bfloat16 [4, 2, 8192, 8, 8, 128], P('pole', None, 'row', None, 'col'), may hold values from -0.125 to 0.125
- l_panel: bfloat16 [4, 2, 8192, 512], P('pole', None, ('row', 'col')), may hold values from -1.5 to 1.5
- block_pattern: int32 [64, 4], P(('row', 'col')), may hold values 0 or 1
- sup_widths: int32 [4], replicated, may hold values from 1 to 128, 320 in all
- diag_inverse: bfloat16 [4, 2, 512, 128], P('pole'), may hold values from -6 to 6
- pole_weights: float32 [4, 2], P('pole'), may hold values from -4 to 4
Outputs:
- density: float32 [512, 8192], P('col', 'row')
- diagonal: float32 [512, 128], replicated
Inputs may be any that keep to these rules, and one draw needn't show every extreme that they name: `sup_widths`: one supernode has exactly 128 columns.
All inputs are finite; a program needn't handle non-finite values. No bound on the sum of `block_pattern` on one device may be relied on, other than what follows from the above.
Results may differ from a plain program's by a relative error of at most 0.0003.
Values may be sent and summed in bfloat16 or wider, within the bound.
A program may use at most 128 MiB of HBM per device.

v0:
```python
import jax
import jax.numpy as jnp
from jax import lax
from jax.sharding import PartitionSpec as P


def contract(left, right):
    return jnp.einsum("jk,ij->ki", left, right, preferred_element_type=jnp.float32)


def pair_product(left, right):
    return jnp.einsum("ika,kbi->kab", left, right, precision=lax.Precision.HIGHEST)


def per_device(found_inverse, l_panel, block_pattern, sup_widths, diag_inverse, pole_weights):
    slot_width = diag_inverse.shape[-1]
    total_cols = l_panel.shape[-1]
    supernodes = total_cols // slot_width
    row_count = lax.axis_size("row")
    row_index = lax.axis_index("row")
    col_index = lax.axis_index("col")
    columns = jnp.arange(total_cols, dtype=jnp.int32)
    column_ok = columns % slot_width < jnp.repeat(sup_widths, slot_width)
    block_ok = jnp.repeat(block_pattern[0], slot_width) == 1
    masked = jnp.where(
        (column_ok & block_ok)[None, None, :], l_panel[0], jnp.zeros((), jnp.bfloat16)
    )
    column_rows = lax.all_gather(masked, "row", axis=1, tiled=True)
    own_rows = lax.all_gather(masked, "col", axis=1, tiled=True)
    local_rows = found_inverse.shape[2]
    inverse = found_inverse[0].reshape(2, local_rows, row_count * slot_width)
    part_real = contract(column_rows[1], inverse[1]) - contract(column_rows[0], inverse[0])
    part_imag = -(contract(column_rows[1], inverse[0]) + contract(column_rows[0], inverse[1]))
    w_real = pole_weights[0, 0]
    w_imag = pole_weights[0, 1]
    weighted = w_real * part_real - w_imag * part_imag
    part = lax.psum_scatter(weighted, "col", scatter_dimension=0, tiled=True)
    density = lax.psum(part, "pole")
    lifted = own_rows.astype(jnp.float32).reshape(2, local_rows, supernodes, slot_width)
    upper_real = part_real.reshape(supernodes, slot_width, local_rows)
    upper_imag = part_imag.reshape(supernodes, slot_width, local_rows)
    t_real = pair_product(lifted[0], upper_real) - pair_product(lifted[1], upper_imag)
    t_imag = pair_product(lifted[0], upper_imag) + pair_product(lifted[1], upper_real)
    lead_flag = ((row_index == 0) & (col_index == 0)).astype(jnp.float32)
    d_real = diag_inverse[0, 0].astype(jnp.float32).reshape(supernodes, slot_width, slot_width)
    d_imag = diag_inverse[0, 1].astype(jnp.float32).reshape(supernodes, slot_width, slot_width)
    local_term = lead_flag * (w_real * d_real - w_imag * d_imag) - (
        w_real * t_real - w_imag * t_imag
    )
    diagonal = lax.psum(local_term.reshape(total_cols, slot_width), ("pole", "row", "col"))
    return (density, diagonal)


def solution(mesh):
    in_specs = (
        P("pole", None, "row", None, "col", None),
        P("pole", None, ("row", "col"), None),
        P(("row", "col"), None),
        P(),
        P("pole", None, None, None),
        P("pole", None),
    )
    out_specs = (P("col", "row"), P())
    return jax.shard_map(
        per_device, mesh=mesh, in_specs=in_specs, out_specs=out_specs, check_vma=False
    )
```

profile of v0, /device:TPU:2, one launch (start us, length us, event | category | flops | bytes accessed | tf_op | source)
XLA Modules:
  0.0 457.6 jit_solution(11535285280863356408)
XLA Ops:
  7.2 0.0 all-gather.3.cloned.1.call-start
  7.2 0.7 compare_bitcast_fusion
  7.9 0.7 fusion.25
  8.6 1.7 bitcast_select_fusion
  10.3 0.0 all-gather.3.cloned.1.call-update
  10.3 0.0 all-gather.5.cloned.1.call-start
  10.3 0.7 all-gather.5.cloned.1.call-update
  11.1 0.0 reduce-scatter.2.cloned.1.call-start
  11.1 1.4 fusion.28
  12.5 3.8 fusion.26
  16.3 38.6 %all-gather.3.cloned.1.call-done = bf16[2,1024,512]{2,1,0:T(8,128)(2,1)} async-done(((bf16[2,128,512]{2,1,0:T(8,128)(2,1)}), bf16[2,1024,512]{2,1,0:T(8,128)(2,1)}) %all-gather.3.cloned.1.call-update) | async-done | bytes 2097168 | tf_op jit(solution)/shard_map/all_gather | solution.py:28
  54.9 0.0 copy-start.3
  54.9 2.7 fusion.2
  57.6 0.0 copy-done.3
  57.6 0.0 copy-start.2
  57.6 1.3 fusion
  58.9 0.3 copy-done.2
  59.2 1.3 fusion.12
  60.5 4.6 %multiply_subtract_fusion = (f32[512,1024]{1,0:T(8,128)}, f32[512,1024]{1,0:T(8,128)}) fusion(f32[512,1024]{1,0:T(8,128)S(1)} %fusion.12, f32[]{:T(128)} %bitcast.7, f32[]{:T(128)} %bitcast, f32[512,1024]{1,0:T(8,128)S(1)} %fusion, bf16[128,8,8,128]{3,2,1,0:T(8,128)(2,1)S(1)} %bitcast.67, bf16[2,1024,512]{2,1,0:T(8,128)(2,1)S(1)} %copy-done.3), kind=kOutput, calls=%fused_computation.8 | convolution fusion | flops 1076363264 | bytes 11534344 | tf_op jit(solution)/shard_map/jk,ij->ki/dot_general | solution.py:8
  65.1 0.0 copy-start.4
  65.1 0.0 reduce-scatter.2.cloned.1.call-update
  65.1 0.0 all-reduce.5.cloned.1.call-start
  65.2 0.9 copy-done.4
  66.1 1.3 subtract_multiply_fusion
  67.4 27.9 %all-gather.5.cloned.1.call-done = bf16[2,1024,512]{2,1,0:T(8,128)(2,1)} async-done(((bf16[2,128,512]{2,1,0:T(8,128)(2,1)}), bf16[2,1024,512]{2,1,0:T(8,128)(2,1)}) %all-gather.5.cloned.1.call-update) | async-done | bytes 2097168 | tf_op jit(solution)/shard_map/all_gather | solution.py:29
  95.3 2.7 fusion.27
  97.9 1.3 copy.8
  99.3 1.5 copy.9
  100.8 0.0 copy-start
  100.8 0.0 copy-start.1
  100.8 2.5 fusion.29
  103.3 0.0 copy-done
  103.3 0.0 copy-done.1
  103.3 1.2 fusion.30
  104.5 1.9 fusion.20
  106.4 2.5 fusion.19
  108.9 0.0 all-reduce.5.cloned.1.call-update
  108.9 0.0 all-reduce.3.cloned.1.call-start
  109.0 31.0 %reduce-scatter.2.cloned.1.call-done = f32[64,1024]{1,0:T(8,128)} async-done(((f32[512,1024]{1,0:T(8,128)}), f32[64,1024]{1,0:T(8,128)}) %reduce-scatter.2.cloned.1.call-update) | async-done | bytes 262160 | tf_op jit(solution)/shard_map/reduce_scatter | solution.py:37
  140.0 0.0 all-reduce.3.cloned.1.call-update
  140.1 259.7 %all-reduce.5.cloned.1.call-done = f32[512,128]{1,0:T(8,128)} async-done(((f32[512,128]{1,0:T(8,128)}), f32[512,128]{1,0:T(8,128)}) %all-reduce.5.cloned.1.call-update) | async-done | bytes 262160 | tf_op jit(solution)/shard_map/psum | solution.py:50
  399.8 48.0 %all-reduce.3.cloned.1.call-done = f32[64,1024]{1,0:T(8,128)} async-done(((f32[64,1024]{1,0:T(8,128)}), f32[64,1024]{1,0:T(8,128)}) %all-reduce.3.cloned.1.call-update) | async-done | bytes 262160 | tf_op jit(solution)/shard_map/psum | solution.py:38
  447.8 1.7 copy.36
  449.4 1.7 copy.37
Async XLA Ops:
  7.2 47.7 %all-gather.3.cloned.1.call-start = ((), (), s32[]{:S(2)}) async-start(), calls=%async_computation.1 | async-start | bytes 2359296 | tf_op jit(solution)/shard_map/all_gather | solution.py:28
  10.3 85.0 %all-gather.5.cloned.1.call-start = ((), (), s32[]{:S(2)}) async-start(), calls=%async_computation.4 | async-start | bytes 2359296 | tf_op jit(solution)/shard_map/all_gather | solution.py:29
  11.1 129.0 %reduce-scatter.2.cloned.1.call-start = ((), (), s32[]{:S(2)}) async-start(), calls=%async_computation.2 | async-start | bytes 2359296 | tf_op jit(solution)/shard_map/reduce_scatter | solution.py:37
  54.9 2.7 copy-start.3
  57.6 1.6 copy-start.2
  65.1 0.9 copy-start.4
  65.1 334.7 %all-reduce.5.cloned.1.call-start = ((), (), s32[]{:S(2)}) async-start(), calls=%async_computation.5 | async-start | bytes 524288 | tf_op jit(solution)/shard_map/psum | solution.py:50
  100.8 2.6 copy-start
  100.8 2.6 copy-start.1
  108.9 338.8 %all-reduce.3.cloned.1.call-start = ((), (), s32[]{:S(2)}) async-start(), calls=%async_computation.3 | async-start | bytes 524288 | tf_op jit(solution)/shard_map/psum | solution.py:38
Sparse Core Ops, SparseCore 0:
  10.4 44.4 all-gather.2
  57.3 37.9 all-gather.4
  97.8 42.1 reduce-scatter.1
  145.9 253.8 all-reduce.4
  402.0 45.7 all-reduce.2
where the time goes:
time: 458 us
  waiting for transfers between devices  406 us (89%)
  matrix products  18 us (4%)
  local copies, waits for them, and re-layouts  15.2 us (3%)
  between operations  13.9 us (3%)
    psum x1, waiting for transfers between devices, per_device(): lax.psum(local_term.reshape(total_cols, slot_width), ('pole', 'row', 'col'))  260 us
    psum x1, waiting for transfers between devices, per_device(): density = lax.psum(part, 'pole')  48 us
    all_gather x1, waiting for transfers between devices, per_device(): column_rows = lax.all_gather(masked, 'row', axis=1, tiled=True)  38.6 us
    reduce_scatter x1, waiting for transfers between devices, per_device(): part = lax.psum_scatter(weighted, 'col', scatter_dimension=0, tiled=True)  31 us
    all_gather x1, waiting for transfers between devices, per_device(): own_rows = lax.all_gather(masked, 'col', axis=1, tiled=True)  27.9 us
    dot_general x4, matrix products, contract(): jnp.einsum('jk,ij->ki', left, right, preferred_element_type=jnp.float32)  9.92 us
  transfers between devices with their start and end apart: 5, of which 5 were waited for; matrix products, arithmetic and copies ran while one was open for 7% of the time, Pallas kernels for 0%

commit v1 on v0

--- a/solution.py
+++ b/solution.py
@@ -47,7 +47,9 @@
     local_term = lead_flag * (w_real * d_real - w_imag * d_imag) - (
         w_real * t_real - w_imag * t_imag
     )
-    diagonal = lax.psum(local_term.reshape(total_cols, slot_width), ("pole", "row", "col"))
+    diagonal = lax.psum(
+        lax.psum(local_term.reshape(total_cols, slot_width), ("row", "col")), "pole"
+    )
     return (density, diagonal)
 
 

time: 458 us -> 393 us (0.86)
  waiting for transfers between devices: 406 us -> 344 us
    psum x1, waiting for transfers between devices: 260 us -> 177 us  [per_device(): lax.psum(local_term.reshape(total_cols, slot_width), ('row', 'col'))]
    reduce_scatter x1, waiting for transfers between devices: 31 us -> 45 us  [per_device(): part = lax.psum_scatter(weighted, 'col', scatter_dimension=0, tiled=True)]
  transfers between devices with their start and end apart: 5 -> 5, of which waited for: 5 -> 5; matrix products, arithmetic and copies ran while one was open for 7% -> 3% of each run, Pallas kernels for 0% -> 0%
where the time goes in v1:
time: 393 us; the launch traced here: 392 us
  waiting for transfers between devices  344 us (88%)
  matrix products  16.6 us (4%)
  between operations  13.9 us (4%)
  local copies, waits for them, and re-layouts  12.3 us (3%)
  other arithmetic  5.35 us (1%)
    psum x1, waiting for transfers between devices, per_device(): lax.psum(local_term.reshape(total_cols, slot_width), ('row', 'col'))  177 us
    psum x1, waiting for transfers between devices, per_device(): density = lax.psum(part, 'pole')  50.6 us
    reduce_scatter x1, waiting for transfers between devices, per_device(): part = lax.psum_scatter(weighted, 'col', scatter_dimension=0, tiled=True)  45 us
    all_gather x1, waiting for transfers between devices, per_device(): column_rows = lax.all_gather(masked, 'row', axis=1, tiled=True)  39.4 us
    all_gather x1, waiting for transfers between devices, per_device(): own_rows = lax.all_gather(masked, 'col', axis=1, tiled=True)  30.4 us
    dot_general x4, matrix products, contract(): jnp.einsum('jk,ij->ki', left, right, preferred_element_type=jnp.float32)  9.97 us
  transfers between devices with their start and end apart: 5, of which 5 were waited for; matrix products, arithmetic and copies ran while one was open for 3% of the time, Pallas kernels for 0%

profile of v1, /device:TPU:2, one launch (start us, length us, event | category | flops | bytes accessed | tf_op | source)
XLA Modules:
  0.0 392.4 jit_solution(14994705129801200079)
XLA Ops:
  7.2 0.0 all-gather.5.cloned.1.call-start
  7.2 0.7 compare_bitcast_fusion
  7.9 0.7 fusion.25
  8.6 1.7 bitcast_select_fusion
  10.3 0.0 all-gather.5.cloned.1.call-update
  10.3 0.0 all-gather.3.cloned.1.call-start
  10.3 0.7 all-gather.3.cloned.1.call-update
  11.1 0.0 all-reduce.4.cloned.1.call-start
  11.1 1.3 fusion.28
  12.4 2.3 subtract_multiply_fusion
  14.7 4.5 %fusion.26 = (bf16[1,1,1024,8,1,128]{5,3,4,2,1,0:T(8,128)(2,1)}, bf16[1,1,1024,8,1,128]{5,3,4,2,1,0:T(8,128)(2,1)}) fusion(bf16[1,2,1024,8,1,128]{5,3,4,2,1,0:T(8,128)(2,1)} %param.6), kind=kLoop, calls=%fused_computation.33 | loop fusion | bytes 8388608 | tf_op jit(solution)/shard_map/slice | solution.py:32
  19.2 30.4 %all-gather.5.cloned.1.call-done = bf16[2,1024,512]{2,1,0:T(8,128)(2,1)} async-done(((bf16[2,128,512]{2,1,0:T(8,128)(2,1)}), bf16[2,1024,512]{2,1,0:T(8,128)(2,1)}) %all-gather.5.cloned.1.call-update) | async-done | bytes 2097168 | tf_op jit(solution)/shard_map/all_gather | solution.py:29
  49.6 1.7 fusion.27
  51.3 0.5 copy.8
  51.9 0.5 copy.9
  52.4 39.4 %all-gather.3.cloned.1.call-done = bf16[2,1024,512]{2,1,0:T(8,128)(2,1)} async-done(((bf16[2,128,512]{2,1,0:T(8,128)(2,1)}), bf16[2,1024,512]{2,1,0:T(8,128)(2,1)}) %all-gather.3.cloned.1.call-update) | async-done | bytes 2097168 | tf_op jit(solution)/shard_map/all_gather | solution.py:28
  91.8 0.0 copy-start
  91.8 0.0 copy-start.2
  91.8 3.4 fusion.2
  95.2 0.0 copy-done
  95.2 0.0 copy-done.2
  95.2 1.3 fusion.12
  96.5 0.0 copy-start.1
  96.5 1.2 fusion.29
  97.7 0.4 copy-done.1
  98.1 1.3 fusion
  99.4 4.0 %multiply_subtract_fusion = (f32[512,1024]{1,0:T(8,128)}, f32[512,1024]{1,0:T(8,128)S(1)}) fusion(f32[512,1024]{1,0:T(8,128)S(1)} %fusion.12, f32[]{:T(128)} %bitcast.7, f32[]{:T(128)} %bitcast, f32[512,1024]{1,0:T(8,128)S(1)} %fusion, bf16[128,8,8,128]{3,2,1,0:T(8,128)(2,1)S(1)} %bitcast.67, bf16[2,1024,512]{2,1,0:T(8,128)(2,1)S(1)} %copy-done.2), kind=kOutput, calls=%fused_computation.8 | convolution fusion | flops 1076363264 | bytes 11534344 | tf_op jit(solution)/shard_map/jk,ij->ki/dot_general | solution.py:8
  103.4 1.2 fusion.30
  104.6 1.8 fusion.20
  106.4 2.5 fusion.19
  108.9 0.0 all-reduce.4.cloned.1.call-update
  108.9 0.0 reduce-scatter.2.cloned.1.call-start
  109.0 0.5 reduce-scatter.2.cloned.1.call-update
  109.5 0.0 all-reduce.6.cloned.1.call-start
  109.6 177.4 %all-reduce.4.cloned.1.call-done = f32[512,128]{1,0:T(8,128)} async-done(((f32[512,128]{1,0:T(8,128)}), f32[512,128]{1,0:T(8,128)}) %all-reduce.4.cloned.1.call-update) | async-done | bytes 262160 | tf_op jit(solution)/shard_map/psum | solution.py:51
  287.0 45.0 %reduce-scatter.2.cloned.1.call-done = f32[64,1024]{1,0:T(8,128)} async-done(((f32[512,1024]{1,0:T(8,128)}), f32[64,1024]{1,0:T(8,128)}) %reduce-scatter.2.cloned.1.call-update) | async-done | bytes 262160 | tf_op jit(solution)/shard_map/reduce_scatter | solution.py:37
  332.0 0.0 all-reduce.6.cloned.1.call-update
  332.0 50.6 %all-reduce.6.cloned.1.call-done = (f32[64,1024]{1,0:T(8,128)}, f32[512,128]{1,0:T(8,128)}) async-done(((f32[64,1024]{1,0:T(8,128)}, f32[512,128]{1,0:T(8,128)}), (f32[64,1024]{1,0:T(8,128)}, f32[512,128]{1,0:T(8,128)})) %all-reduce.6.cloned.1.call-update) | async-done | bytes 524304 | tf_op jit(solution)/shard_map/psum | solution.py:38
  382.6 1.7 copy.37
  384.2 1.7 copy.38
Async XLA Ops:
  7.2 42.5 %all-gather.5.cloned.1.call-start = ((), (), s32[]{:S(2)}) async-start(), calls=%async_computation.3 | async-start | bytes 2359296 | tf_op jit(solution)/shard_map/all_gather | solution.py:29
  10.3 81.5 %all-gather.3.cloned.1.call-start = ((), (), s32[]{:S(2)}) async-start(), calls=%async_computation.1 | async-start | bytes 2359296 | tf_op jit(solution)/shard_map/all_gather | solution.py:28
  11.1 275.9 %all-reduce.4.cloned.1.call-start = ((), (), s32[]{:S(2)}) async-start(), calls=%async_computation.4 | async-start | bytes 524288 | tf_op jit(solution)/shard_map/psum | solution.py:51
  91.8 3.4 copy-start
  91.8 3.4 copy-start.2
  96.5 1.6 copy-start.1
  108.9 223.0 %reduce-scatter.2.cloned.1.call-start = ((), (), s32[]{:S(2)}) async-start(), calls=%async_computation.2 | async-start | bytes 2359296 | tf_op jit(solution)/shard_map/reduce_scatter | solution.py:37
  109.5 273.0 %all-reduce.6.cloned.1.call-start = ((), (), s32[]{:S(2)}) async-start(), calls=%async_computation.5 | async-start | bytes 1048576 | tf_op jit(solution)/shard_map/psum | solution.py:38
Sparse Core Ops, SparseCore 0:
  10.4 39.1 all-gather.4
  52.0 39.7 all-gather.2
  109.1 177.8 all-reduce.3
  289.4 42.5 reduce-scatter.1
  334.2 48.2 all-reduce.5
